TPU v7x, 256 devices: a whole 4x4x8 slice. The times are simulated.
256 devices in a mesh: seq: 16 (over z, core), fsdp: 16 (over x, y).
Axes of the slice: x: 4, y: 4, z: 8, core: 2. Of those that a mesh axis runs over, the one named last changes fastest.
Arguments:
- inputs: bfloat16 [16, 2048, 2304], P('fsdp', 'seq'), may hold values from -6 to 6
- queries: bfloat16 [16, 2048, 2048], P('fsdp', 'seq'), may hold values from -96 to 96
- w_kv: bfloat16 [2304, 2048], P('fsdp'), may hold values from -0.125 to 0.125
- doc_lengths: int32 [16, 8], P('fsdp'), may hold values from 1 to 1536, 2048 in all within a row
- grad_out: bfloat16 [16, 2048, 2048], P('fsdp', 'seq'), may hold values from -6 to 6
Outputs:
- attn_out: bfloat16 [16, 2048, 2048], P('fsdp', 'seq')
- grad_inputs: bfloat16 [16, 2048, 2304], P('fsdp', 'seq')
- grad_weights: float32 [2304, 2048], P('fsdp', 'seq')
Inputs may be any that keep to these rules, and one draw needn't show every extreme that they name: `doc_lengths`: each row lists the lengths of the 8 documents packed in order into one sequence; a row sums to 2048 and its longest document has 1536 tokens.
All inputs are finite; a program needn't handle non-finite values.
Results may differ from a plain program's by a relative error of at most 0.03.
Values may be sent and summed in bfloat16 or wider, within the bound.
A program may use at most 128 MiB of HBM per device.

v0:
```python
import jax
import jax.numpy as jnp
from jax import lax
from jax.sharding import PartitionSpec as P

QH = 16
KVH = 8
HD = 128
WIN = 1024
G = 2
SOFT_CAP = 50.0
QUERY_SCALE = 1.0 / 12.0
ROPE_BASE = 10000.0


def from_behind(value, axis, steps):
    count = lax.axis_size(axis)
    first, last = (max(0, -steps), min(count, count - steps))
    return lax.ppermute(value, axis, [(source, source + steps) for source in range(first, last)])


def doc_layout(lengths, places):
    doc_ends = jnp.cumsum(lengths)
    doc_ended = doc_ends[None, :] <= places[:, None]
    doc_index = jnp.sum(doc_ended.astype(jnp.int32), axis=1)
    before = jnp.sum(jnp.where(doc_ended, lengths[None, :], 0), axis=1)
    return (doc_index, places - before)


def rotate(values, places, direction):
    half_dim = values.shape[-1] // 2
    exponent = jnp.arange(half_dim, dtype=jnp.float32) * (2.0 / values.shape[-1])
    inverse_rate = jnp.power(ROPE_BASE, -exponent)
    angles = places.astype(jnp.float32)[:, None] * inverse_rate[None, :]
    cosine = jnp.cos(angles)[:, None, :]
    sine_part = direction * jnp.sin(angles)[:, None, :]
    first_half = values[..., :half_dim]
    second_half = values[..., half_dim:]
    return jnp.concatenate(
        [
            first_half * cosine - second_half * sine_part,
            second_half * cosine + first_half * sine_part,
        ],
        axis=-1,
    )


def attend(earlier, query_rows, cotangent, window, allowed):
    row_count = query_rows.shape[0]
    used_rows = (earlier + 1) * row_count
    half_kv = KVH * HD
    pair_width = 2 * G * HD

    def one_pair(pair_index, state_now):
        out_acc, key_acc, value_acc = state_now
        q_part = lax.dynamic_slice_in_dim(
            query_rows, pair_index * pair_width, pair_width, 1
        ).reshape(row_count, 2, G, HD)
        d_part = lax.dynamic_slice_in_dim(
            cotangent, pair_index * pair_width, pair_width, 1
        ).reshape(row_count, 2, G, HD)
        k_part = lax.dynamic_slice_in_dim(window, pair_index * 2 * HD, 2 * HD, 1).reshape(
            used_rows, 2, HD
        )
        v_part = lax.dynamic_slice_in_dim(window, half_kv + pair_index * 2 * HD, 2 * HD, 1).reshape(
            used_rows, 2, HD
        )
        scores = (
            jnp.einsum("tkgd,nkd->kgtn", q_part, k_part, preferred_element_type=jnp.float32)
            * QUERY_SCALE
        )
        squashed = jnp.tanh(scores / SOFT_CAP)
        weights = jnp.where(allowed[None, None], jnp.exp(SOFT_CAP * squashed), 0.0)
        probs = weights / jnp.sum(weights, axis=-1, keepdims=True)
        rounded = probs.astype(jnp.bfloat16)
        attended = jnp.einsum(
            "kgtn,nkd->tkgd", rounded, v_part, preferred_element_type=jnp.float32
        ).astype(jnp.bfloat16)
        delta_row = jnp.einsum(
            "tkgd,tkgd->kgt", d_part, attended, preferred_element_type=jnp.float32
        )
        dprob = jnp.einsum("tkgd,nkd->kgtn", d_part, v_part, preferred_element_type=jnp.float32)
        dscore = (probs * (dprob - delta_row[..., None]) * (1.0 - squashed * squashed)).astype(
            jnp.bfloat16
        )
        key_grad = (
            jnp.einsum("kgtn,tkgd->nkd", dscore, q_part, preferred_element_type=jnp.float32)
            * QUERY_SCALE
        )
        value_grad = jnp.einsum(
            "kgtn,tkgd->nkd", rounded, d_part, preferred_element_type=jnp.float32
        )
        out_acc = lax.dynamic_update_slice_in_dim(
            out_acc, attended.reshape(row_count, pair_width), pair_index * pair_width, 1
        )
        key_acc = lax.dynamic_update_slice_in_dim(
            key_acc, key_grad.reshape(used_rows, 2 * HD), pair_index * 2 * HD, 1
        )
        value_acc = lax.dynamic_update_slice_in_dim(
            value_acc, value_grad.reshape(used_rows, 2 * HD), pair_index * 2 * HD, 1
        )
        return (out_acc, key_acc, value_acc)

    initial = (
        jnp.zeros((row_count, QH * HD), jnp.bfloat16),
        jnp.zeros((used_rows, half_kv), jnp.float32),
        jnp.zeros((used_rows, half_kv), jnp.float32),
    )
    out_rows, key_grads, value_grads = lax.fori_loop(0, KVH // 2, one_pair, initial)
    return (out_rows, key_grads, value_grads)


def on_device(inputs, queries, w_kv, doc_lengths, grad_out):
    tokens = inputs[0]
    query_rows = queries[0]
    cotangent = grad_out[0]
    lengths = doc_lengths[0]
    row_count = tokens.shape[0]
    seq_count = lax.axis_size("seq")
    shard_index = lax.axis_index("seq")
    reach_blocks = min((WIN + row_count - 2) // row_count, seq_count - 1)
    half_kv = KVH * HD
    weight_full = lax.all_gather(w_kv, "fsdp", axis=0, tiled=True)
    projected = jnp.dot(tokens, weight_full, preferred_element_type=jnp.float32)
    places = shard_index * row_count + jnp.arange(row_count, dtype=jnp.int32)
    doc_index, within = doc_layout(lengths, places)
    own_keys = rotate(projected[:, :half_kv].reshape(row_count, KVH, HD), within, 1.0).reshape(
        row_count, half_kv
    )
    own_block = jnp.concatenate([own_keys, projected[:, half_kv:]], axis=1).astype(jnp.bfloat16)
    received = [own_block]
    for offset in range(1, reach_blocks + 1):
        received.append(from_behind(own_block, "seq", offset))
    window = jnp.concatenate(received[::-1], axis=0)
    key_places = (shard_index - reach_blocks) * row_count + jnp.arange(
        (reach_blocks + 1) * row_count, dtype=jnp.int32
    )
    key_doc, ignored = doc_layout(lengths, key_places)
    distance = places[:, None] - key_places[None, :]
    allowed = (
        (key_places[None, :] >= 0)
        & (doc_index[:, None] == key_doc[None, :])
        & (distance >= 0)
        & (distance <= WIN - 1)
    )
    out_rows, key_grads, value_grads = attend(reach_blocks, query_rows, cotangent, window, allowed)
    split_at = reach_blocks * row_count
    remote = jnp.concatenate(
        [key_grads[:split_at].astype(jnp.bfloat16), value_grads[:split_at].astype(jnp.bfloat16)],
        axis=1,
    )
    remote = remote.reshape(reach_blocks, row_count, 2 * half_kv)
    summed = jnp.concatenate([key_grads[split_at:], value_grads[split_at:]], axis=1)
    for offset in range(1, reach_blocks + 1):
        arrived = from_behind(remote[reach_blocks - offset], "seq", -offset)
        summed = summed + arrived.astype(jnp.float32)
    key_total = rotate(summed[:, :half_kv].reshape(row_count, KVH, HD), within, -1.0).reshape(
        row_count, half_kv
    )
    grad_kv = jnp.concatenate([key_total, summed[:, half_kv:]], axis=1).astype(jnp.bfloat16)
    grad_rows = jnp.dot(grad_kv, weight_full.T, preferred_element_type=jnp.float32).astype(
        jnp.bfloat16
    )
    shared = lax.psum_scatter(
        lax.dot_general(
            tokens, grad_kv, (((0,), (0,)), ((), ())), preferred_element_type=jnp.float32
        ).astype(jnp.bfloat16),
        "fsdp",
        scatter_dimension=0,
        tiled=True,
    )
    finished = lax.psum_scatter(shared, "seq", scatter_dimension=1, tiled=True).astype(jnp.float32)
    return (out_rows[None], grad_rows[None], finished)


def solution(mesh):
    in_specs = (
        P("fsdp", "seq", None),
        P("fsdp", "seq", None),
        P("fsdp", None),
        P("fsdp", None),
        P("fsdp", "seq", None),
    )
    out_specs = (P("fsdp", "seq", None), P("fsdp", "seq", None), P("fsdp", "seq"))
    return jax.shard_map(
        on_device, mesh=mesh, in_specs=in_specs, out_specs=out_specs, check_vma=False
    )
```

profile of v0, /device:TPU:4, one launch (start us, length us, event | category | flops | bytes accessed | tf_op | source)
XLA Modules:
  0.0 725.4 jit_solution(4703402251227408415)
XLA Ops:
  11.6 82.5 %all-gather.2.cloned.1.call-done = bf16[2304,2048]{1,0:T(8,128)(2,1)} async-done(((bf16[144,2048]{1,0:T(8,128)(2,1)}), bf16[2304,2048]{1,0:T(8,128)(2,1)}) %all-gather.2.cloned.1.call-update) | async-done | bytes 9437200 | tf_op jit(solution)/shard_map/all_gather | solution.py:123
  94.2 5.1 fusion.32
  100.0 8.5 %collective-permute-start = (bf16[128,2048]{1,0:T(8,128)(2,1)S(1)}, bf16[128,2048]{1,0:T(8,128)(2,1)}, u32[]{:S(2)}, u32[]{:S(2)}) collective-permute-start(bf16[128,2048]{1,0:T(8,128)(2,1)S(1)} %pad_maximum_fusion.1), channel_id=1, source_target_pairs={{0,128},{16,144},{32,160},{48,176},{64,192},{80,208},{96,224},{112... | collective-permute-start | bytes 1572872 | tf_op jit(solution)/shard_map/ppermute | solution.py:19
  111.2 3.0 collective-permute-start.2
  120.1 56.2 %collective-permute-start.3 = (bf16[128,2048]{1,0:T(8,128)(2,1)S(1)}, bf16[128,2048]{1,0:T(8,128)(2,1)S(1)}, u32[]{:S(2)}, u32[]{:S(2)}) collective-permute-start(bf16[128,2048]{1,0:T(8,128)(2,1)S(1)} %pad_maximum_fusion.1), channel_id=1, source_target_pairs={{0,80},{16,96},{32,112},{48,128},{64,144},{80,160},{96,176},{112,1... | collective-permute-start | bytes 1572872 | tf_op jit(solution)/shard_map/ppermute | solution.py:19
  178.2 12.0 %collective-permute-start.4 = (bf16[128,2048]{1,0:T(8,128)(2,1)S(1)}, bf16[128,2048]{1,0:T(8,128)(2,1)S(1)}, u32[]{:S(2)}, u32[]{:S(2)}) collective-permute-start(bf16[128,2048]{1,0:T(8,128)(2,1)S(1)} %pad_maximum_fusion.1), channel_id=1, source_target_pairs={{0,64},{16,80},{32,96},{48,112},{64,128},{80,144},{96,160},{112,17... | collective-permute-start | bytes 1572872 | tf_op jit(solution)/shard_map/ppermute | solution.py:19
  196.2 3.1 collective-permute-done.4
  200.1 6.0 collective-permute-done.5
  209.4 6.7 copy.70
  221.9 72.9 %while.20 = (s32[]{:T(128)}, bf16[128,2048]{1,0:T(8,128)(2,1)}, f32[1152,1024]{0,1:T(8,128)}, f32[1152,1024]{0,1:T(8,128)}, bf16[1152,2048]{0,1:T(8,128)(2,1)}, ...) while((s32[]{:T(128)}, bf16[128,2048]{1,0:T(8,128)(2,1)}, ...), condition=%wide.region_6.7_spmd.clone, body=%wide.region_4.6_spmd.clone.sunk | while | flops 766655488 | bytes 39024268 | solution.py:109
  232.3 3.1 fusion.87
  250.5 3.1 fusion.87
  268.7 3.1 fusion.87
  287.0 3.1 fusion.87
  299.9 2.8 fusion.35
  311.9 47.2 %collective-permute-done.9 = bf16[128,2048]{0,1:T(8,128)(2,1)S(1)} collective-permute-done((bf16[128,2048]{0,1:T(8,128)(2,1)S(1)}, bf16[128,2048]{0,1:T(8,128)(2,1)S(1)}, u32[]{:S(2)}, u32[]{:S(2)}) %collective-permute-start.9) | collective-permute-done | bytes 524320 | tf_op jit(solution)/shard_map/ppermute | solution.py:19
  364.3 62.7 %collective-permute-done.11 = bf16[128,2048]{0,1:T(8,128)(2,1)S(1)} collective-permute-done((bf16[128,2048]{0,1:T(8,128)(2,1)S(1)}, bf16[128,2048]{0,1:T(8,128)(2,1)S(1)}, u32[]{:S(2)}, u32[]{:S(2)}) %collective-permute-start.11) | collective-permute-done | bytes 524320 | tf_op jit(solution)/shard_map/ppermute | solution.py:19
  427.1 13.7 %collective-permute-done.12 = bf16[128,2048]{0,1:T(8,128)(2,1)S(1)} collective-permute-done((bf16[128,2048]{0,1:T(8,128)(2,1)S(1)}, bf16[128,2048]{0,1:T(8,128)(2,1)S(1)}, u32[]{:S(2)}, u32[]{:S(2)}) %collective-permute-start.12) | collective-permute-done | bytes 524320 | tf_op jit(solution)/shard_map/ppermute | solution.py:19
  440.8 46.6 %collective-permute-done.13 = bf16[128,2048]{0,1:T(8,128)(2,1)S(1)} collective-permute-done((bf16[128,2048]{0,1:T(8,128)(2,1)S(1)}, bf16[128,2048]{0,1:T(8,128)(2,1)S(1)}, u32[]{:S(2)}, u32[]{:S(2)}) %collective-permute-start.13) | collective-permute-done | bytes 524320 | tf_op jit(solution)/shard_map/ppermute | solution.py:19
  490.5 6.5 fusion.22
  497.1 12.7 %copy.97 = bf16[2304,2048]{1,0:T(8,128)(2,1)} copy(bf16[2304,2048]{0,1:T(8,128)(2,1)} %fusion.22) | data formatting | bytes 18874368
  509.9 147.5 %reduce-scatter.7.cloned.1.call-done = bf16[144,2048]{1,0:T(8,128)(2,1)} async-done(((bf16[2304,2048]{1,0:T(8,128)(2,1)}), bf16[144,2048]{1,0:T(8,128)(2,1)}) %reduce-scatter.7.cloned.1.call-update) | async-done | bytes 589840
  659.6 7.8 %fusion.23 = bf16[1,128,2304]{2,1,0:T(8,128)(2,1)} fusion(bf16[2304,2048]{1,0:T(8,128)(2,1)} %all-gather.2.cloned.1.call-done, bf16[128,1024]{0,1:T(8,128)(2,1)S(1)} %slice.169, bf16[128,1024]{0,1:T(8,128)(2,1)S(1)} %bitcast.165), kind=kOutput, calls=%fused_computation.55 | convolution fusion | flops 1209303040 | bytes 10551296 | tf_op jit(solution)/shard_map/dot_general | solution.py:161
  667.4 50.0 %reduce-scatter.5.cloned.1.call-done = bf16[144,128]{0,1:T(8,128)(2,1)} async-done(((bf16[144,2048]{0,1:T(8,128)(2,1)}), bf16[144,128]{0,1:T(8,128)(2,1)}) %reduce-scatter.5.cloned.1.call-update) | async-done | bytes 36880 | tf_op jit(solution)/shard_map/reduce_scatter | solution.py:172
  (177 shorter events, 117.9 us)
Async XLA Ops:
  7.2 87.0 %copy-start = (bf16[1,128,2304]{2,1,0:T(8,128)(2,1)S(1)}, bf16[1,128,2304]{2,1,0:T(8,128)(2,1)}, u32[]{:S(2)}) copy-start(bf16[1,128,2304]{2,1,0:T(8,128)(2,1)} %param.7) | copy-start | bytes 1769476
  7.2 87.0 %all-gather.2.cloned.1.call-start = ((), (), s32[]{:S(2)}) async-start(), calls=%async_computation.2 | async-start | bytes 10027008 | tf_op jit(solution)/shard_map/all_gather | solution.py:123
  7.9 649.5 %reduce-scatter.7.cloned.1.call-start = ((), (), s32[]{:S(2)}) async-start(), calls=%async_computation.4 | async-start | bytes 10027008
  11.6 87.8 %copy-start.6 = (f32[128,64]{1,0:T(8,128)}, f32[128,64]{1,0:T(8,128)S(1)}, u32[]{:S(2)}) copy-start(f32[128,64]{1,0:T(8,128)S(1)} %get-tuple-element.364) | copy-start | bytes 98308
  99.3 15.8 %copy-start.9 = (bf16[1,128,2048]{2,1,0:T(8,128)(2,1)S(1)}, bf16[1,128,2048]{2,1,0:T(8,128)(2,1)}, u32[]{:S(2)}) copy-start(bf16[1,128,2048]{2,1,0:T(8,128)(2,1)} %param.11) | copy-start | bytes 1572868
  100.0 20.1 %collective-permute-start = (bf16[128,2048]{1,0:T(8,128)(2,1)S(1)}, bf16[128,2048]{1,0:T(8,128)(2,1)}, u32[]{:S(2)}, u32[]{:S(2)}) collective-permute-start(bf16[128,2048]{1,0:T(8,128)(2,1)S(1)} %pad_maximum_fusion.1), channel_id=1, source_target_pairs={{0,128},{16,144},{32,160},{48,176},{64,192},{80,208},{96,224},{112... | collective-permute-start | bytes 1572872 | tf_op jit(solution)/shard_map/ppermute | solution.py:19
  108.5 69.7 %collective-permute-start.1 = (bf16[128,2048]{1,0:T(8,128)(2,1)S(1)}, bf16[128,2048]{1,0:T(8,128)(2,1)}, u32[]{:S(2)}, u32[]{:S(2)}) collective-permute-start(bf16[128,2048]{1,0:T(8,128)(2,1)S(1)} %pad_maximum_fusion.1), channel_id=1, source_target_pairs={{0,112},{16,128},{32,144},{48,160},{64,176},{80,192},{96,208},{112... | collective-permute-start | bytes 1572872 | tf_op jit(solution)/shard_map/ppermute | solution.py:19
  111.2 80.9 %collective-permute-start.2 = (bf16[128,2048]{1,0:T(8,128)(2,1)S(1)}, bf16[128,2048]{1,0:T(8,128)(2,1)}, u32[]{:S(2)}, u32[]{:S(2)}) collective-permute-start(bf16[128,2048]{1,0:T(8,128)(2,1)S(1)} %pad_maximum_fusion.1), channel_id=1, source_target_pairs={{0,96},{16,112},{32,128},{48,144},{64,160},{80,176},{96,192},{112,... | collective-permute-start | bytes 1572872 | tf_op jit(solution)/shard_map/ppermute | solution.py:19
  116.1 91.7 %collective-permute-start.7 = (bf16[128,2048]{1,0:T(8,128)(2,1)S(1)}, bf16[128,2048]{1,0:T(8,128)(2,1)S(1)}, u32[]{:S(2)}, u32[]{:S(2)}) collective-permute-start(bf16[128,2048]{1,0:T(8,128)(2,1)S(1)} %pad_maximum_fusion.1), channel_id=1, source_target_pairs={{0,16},{16,32},{32,48},{48,64},{64,80},{80,96},{96,112},{112,128},... | collective-permute-start | bytes 1572872 | tf_op jit(solution)/shard_map/ppermute | solution.py:19
  117.4 89.5 %collective-permute-start.6 = (bf16[128,2048]{1,0:T(8,128)(2,1)S(1)}, bf16[128,2048]{1,0:T(8,128)(2,1)S(1)}, u32[]{:S(2)}, u32[]{:S(2)}) collective-permute-start(bf16[128,2048]{1,0:T(8,128)(2,1)S(1)} %pad_maximum_fusion.1), channel_id=1, source_target_pairs={{0,32},{16,48},{32,64},{48,80},{64,96},{80,112},{96,128},{112,144}... | collective-permute-start | bytes 1572872 | tf_op jit(solution)/shard_map/ppermute | solution.py:19
  120.1 75.3 %collective-permute-start.3 = (bf16[128,2048]{1,0:T(8,128)(2,1)S(1)}, bf16[128,2048]{1,0:T(8,128)(2,1)S(1)}, u32[]{:S(2)}, u32[]{:S(2)}) collective-permute-start(bf16[128,2048]{1,0:T(8,128)(2,1)S(1)} %pad_maximum_fusion.1), channel_id=1, source_target_pairs={{0,80},{16,96},{32,112},{48,128},{64,144},{80,160},{96,176},{112,1... | collective-permute-start | bytes 1572872 | tf_op jit(solution)/shard_map/ppermute | solution.py:19
  178.2 21.1 %collective-permute-start.4 = (bf16[128,2048]{1,0:T(8,128)(2,1)S(1)}, bf16[128,2048]{1,0:T(8,128)(2,1)S(1)}, u32[]{:S(2)}, u32[]{:S(2)}) collective-permute-start(bf16[128,2048]{1,0:T(8,128)(2,1)S(1)} %pad_maximum_fusion.1), channel_id=1, source_target_pairs={{0,64},{16,80},{32,96},{48,112},{64,128},{80,144},{96,160},{112,17... | collective-permute-start | bytes 1572872 | tf_op jit(solution)/shard_map/ppermute | solution.py:19
  192.1 14.0 %collective-permute-start.5 = (bf16[128,2048]{1,0:T(8,128)(2,1)S(1)}, bf16[128,2048]{1,0:T(8,128)(2,1)S(1)}, u32[]{:S(2)}, u32[]{:S(2)}) collective-permute-start(bf16[128,2048]{1,0:T(8,128)(2,1)S(1)} %pad_maximum_fusion.1), channel_id=1, source_target_pairs={{0,48},{16,64},{32,80},{48,96},{64,112},{80,128},{96,144},{112,160... | collective-permute-start | bytes 1572872 | tf_op jit(solution)/shard_map/ppermute | solution.py:19
  302.7 7.9 %collective-permute-start.8 = (bf16[128,2048]{0,1:T(8,128)(2,1)S(1)}, bf16[128,2048]{0,1:T(8,128)(2,1)S(1)}, u32[]{:S(2)}, u32[]{:S(2)}) collective-permute-start(bf16[128,2048]{0,1:T(8,128)(2,1)S(1)} %get-tuple-element.348), channel_id=1, source_target_pairs={{16,0},{32,16},{48,32},{64,48},{80,64},{96,80},{112,96},{128,112},... | collective-permute-start | bytes 1572872 | tf_op jit(solution)/shard_map/ppermute | solution.py:19
  304.0 55.1 %collective-permute-start.9 = (bf16[128,2048]{0,1:T(8,128)(2,1)S(1)}, bf16[128,2048]{0,1:T(8,128)(2,1)S(1)}, u32[]{:S(2)}, u32[]{:S(2)}) collective-permute-start(bf16[128,2048]{0,1:T(8,128)(2,1)S(1)} %get-tuple-element.349), channel_id=1, source_target_pairs={{32,0},{48,16},{64,32},{80,48},{96,64},{112,80},{128,96},{144,112}... | collective-permute-start | bytes 1572872 | tf_op jit(solution)/shard_map/ppermute | solution.py:19
  305.3 55.6 %collective-permute-start.10 = (bf16[128,2048]{0,1:T(8,128)(2,1)S(1)}, bf16[128,2048]{0,1:T(8,128)(2,1)S(1)}, u32[]{:S(2)}, u32[]{:S(2)}) collective-permute-start(bf16[128,2048]{0,1:T(8,128)(2,1)S(1)} %get-tuple-element.350), channel_id=1, source_target_pairs={{48,0},{64,16},{80,32},{96,48},{112,64},{128,80},{144,96},{160,112... | collective-permute-start | bytes 1572872 | tf_op jit(solution)/shard_map/ppermute | solution.py:19
  306.7 120.3 %collective-permute-start.11 = (bf16[128,2048]{0,1:T(8,128)(2,1)S(1)}, bf16[128,2048]{0,1:T(8,128)(2,1)S(1)}, u32[]{:S(2)}, u32[]{:S(2)}) collective-permute-start(bf16[128,2048]{0,1:T(8,128)(2,1)S(1)} %get-tuple-element.351), channel_id=1, source_target_pairs={{64,0},{80,16},{96,32},{112,48},{128,64},{144,80},{160,96},{176,11... | collective-permute-start | bytes 1572872 | tf_op jit(solution)/shard_map/ppermute | solution.py:19
  308.0 132.7 %collective-permute-start.12 = (bf16[128,2048]{0,1:T(8,128)(2,1)S(1)}, bf16[128,2048]{0,1:T(8,128)(2,1)S(1)}, u32[]{:S(2)}, u32[]{:S(2)}) collective-permute-start(bf16[128,2048]{0,1:T(8,128)(2,1)S(1)} %get-tuple-element.352), channel_id=1, source_target_pairs={{80,0},{96,16},{112,32},{128,48},{144,64},{160,80},{176,96},{192,1... | collective-permute-start | bytes 1572872 | tf_op jit(solution)/shard_map/ppermute | solution.py:19
  310.6 176.8 %collective-permute-start.13 = (bf16[128,2048]{0,1:T(8,128)(2,1)S(1)}, bf16[128,2048]{0,1:T(8,128)(2,1)S(1)}, u32[]{:S(2)}, u32[]{:S(2)}) collective-permute-start(bf16[128,2048]{0,1:T(8,128)(2,1)S(1)} %get-tuple-element.353), channel_id=1, source_target_pairs={{96,0},{112,16},{128,32},{144,48},{160,64},{176,80},{192,96},{208,... | collective-permute-start | bytes 1572872 | tf_op jit(solution)/shard_map/ppermute | solution.py:19
  359.1 128.3 %collective-permute-start.15 = (bf16[128,2048]{0,1:T(8,128)(2,1)S(1)}, bf16[128,2048]{0,1:T(8,128)(2,1)S(1)}, u32[]{:S(2)}, u32[]{:S(2)}) collective-permute-start(bf16[128,2048]{0,1:T(8,128)(2,1)S(1)} %get-tuple-element.354), channel_id=1, source_target_pairs={{128,0},{144,16},{160,32},{176,48},{192,64},{208,80},{224,96},{240... | collective-permute-start | bytes 1572872 | tf_op jit(solution)/shard_map/ppermute | solution.py:19
  360.9 128.0 %collective-permute-start.14 = (bf16[128,2048]{0,1:T(8,128)(2,1)S(1)}, bf16[128,2048]{0,1:T(8,128)(2,1)S(1)}, u32[]{:S(2)}, u32[]{:S(2)}) collective-permute-start(bf16[128,2048]{0,1:T(8,128)(2,1)S(1)} %get-tuple-element.355), channel_id=1, source_target_pairs={{112,0},{128,16},{144,32},{160,48},{176,64},{192,80},{208,96},{224... | collective-permute-start | bytes 1572872 | tf_op jit(solution)/shard_map/ppermute | solution.py:19
  364.3 125.7 %copy-start.7 = (f32[128,64]{1,0:T(8,128)S(1)}, f32[128,64]{1,0:T(8,128)}, u32[]{:S(2)}) copy-start(f32[128,64]{1,0:T(8,128)} %copy-done.6) | copy-start | bytes 98308
  364.3 125.7 %copy-start.10 = (f32[128,64]{1,0:T(8,128)S(1)}, f32[128,64]{1,0:T(8,128)}, u32[]{:S(2)}) copy-start(f32[128,64]{1,0:T(8,128)} %get-tuple-element.362) | copy-start | bytes 98308
  509.8 207.5 %reduce-scatter.5.cloned.1.call-start = ((), (), s32[]{:S(2)}) async-start(), calls=%async_computation.3 | async-start | bytes 1114112 | tf_op jit(solution)/shard_map/reduce_scatter | solution.py:172
  (25 other events, 86.9 us)
Sparse Core Ops, SparseCore 0:
  10.5 83.6 all-gather.1
  509.9 147.4 reduce-scatter.6
  660.1 57.2 reduce-scatter.4
where the time goes:
time: 727 us; the launch traced here: 725 us
  waiting for transfers between devices  464 us (64%)
  starting transfers between devices  97.3 us (13%)
  local copies, waits for them, and re-layouts  79.2 us (11%)
  matrix products  42.6 us (6%)
  other arithmetic  27.7 us (4%)
  between operations  14.1 us (2%)
    ppermute x16, waiting for transfers between devices, from_behind(): lax.ppermute(value, axis, [(source, source + steps) for source in range(f...  183 us
    unnamed x4, waiting for transfers between devices  148 us
    ppermute x16, starting transfers between devices, from_behind(): lax.ppermute(value, axis, [(source, source + steps) for source in range(f...  97.2 us
    all_gather x1, waiting for transfers between devices, on_device(): weight_full = lax.all_gather(w_kv, 'fsdp', axis=0, tiled=True)  82.5 us
    reduce_scatter x1, waiting for transfers between devices, on_device(): lax.psum_scatter(shared, 'seq', scatter_dimension=1, tiled=True)  50 us
    unnamed x31, local copies, waits for them, and re-layouts  35 us
  transfers between devices with their start and end apart: 19, of which 13 were waited for; matrix products, arithmetic and copies ran while one was open for 3% of the time, Pallas kernels for 0%

commit v1 on v0

--- a/solution.py
+++ b/solution.py
@@ -1,3 +1,4 @@
+import functools
 import jax
 import jax.numpy as jnp
 from jax import lax
@@ -11,6 +12,17 @@
 SOFT_CAP = 50.0
 QUERY_SCALE = 1.0 / 12.0
 ROPE_BASE = 10000.0
+
+
+def serve_thing(sample, which_dim):
+    s_next = jnp.concatenate(
+        lax.all_to_all(jnp.stack([sample] * lax.axis_size("fsdp"), axis=0), "fsdp", 0, 0),
+        axis=which_dim,
+    )
+    return s_next
+
+
+modes_pair = functools.partial(serve_thing, which_dim=0)
 
 
 def from_behind(value, axis, steps):
@@ -120,7 +132,7 @@
     shard_index = lax.axis_index("seq")
     reach_blocks = min((WIN + row_count - 2) // row_count, seq_count - 1)
     half_kv = KVH * HD
-    weight_full = lax.all_gather(w_kv, "fsdp", axis=0, tiled=True)
+    weight_full = modes_pair(w_kv)
     projected = jnp.dot(tokens, weight_full, preferred_element_type=jnp.float32)
     places = shard_index * row_count + jnp.arange(row_count, dtype=jnp.int32)
     doc_index, within = doc_layout(lengths, places)

time: 727 us -> 826 us (1.14)
  waiting for transfers between devices: 464 us -> 549 us
    all_to_all x0 -> x1, waiting for transfers between devices: none -> 145 us  [serve_thing(): lax.all_to_all(jnp.stack([sample] * lax.axis_size('fsdp'), axis=0), 'fsdp...]
    all_gather x1 -> x0, waiting for transfers between devices: 82.5 us -> none  [on_device(): weight_full = lax.all_gather(w_kv, 'fsdp', axis=0, tiled=True)]
    unnamed x4 -> x3, waiting for transfers between devices: 148 us -> 171 us
    unnamed x31 -> x33, local copies, waits for them, and re-layouts: 35 us -> 35 us
where the time goes in v1:
time: 826 us; the launch traced here: 824 us
  waiting for transfers between devices  549 us (66%)
  starting transfers between devices  105 us (13%)
  local copies, waits for them, and re-layouts  85.2 us (10%)
  matrix products  42.5 us (5%)
  other arithmetic  27 us (3%)
  between operations  14.4 us (2%)
    ppermute x16, waiting for transfers between devices, from_behind(): lax.ppermute(value, axis, [(source, source + steps) for source in range(f...  183 us
    unnamed x3, waiting for transfers between devices  171 us
    all_to_all x1, waiting for transfers between devices, serve_thing(): lax.all_to_all(jnp.stack([sample] * lax.axis_size('fsdp'), axis=0), 'fsdp...  145 us
    ppermute x16, starting transfers between devices, from_behind(): lax.ppermute(value, axis, [(source, source + steps) for source in range(f...  97.4 us
    reduce_scatter x1, waiting for transfers between devices, on_device(): lax.psum_scatter(shared, 'seq', scatter_dimension=1, tiled=True)  49.9 us
    unnamed x33, local copies, waits for them, and re-layouts  35 us
  transfers between devices with their start and end apart: 19, of which 13 were waited for; matrix products, arithmetic and copies ran while one was open for 3% of the time, Pallas kernels for 0%

profile of v1, /device:TPU:4, one launch (start us, length us, event | category | flops | bytes accessed | tf_op | source)
XLA Modules:
  0.0 823.9 jit_solution(10230815314534987338)
XLA Ops:
  7.2 6.0 stack.2
  13.2 7.6 all-to-all-start
  23.8 145.5 %all-to-all-done = bf16[16,144,2048]{2,1,0:T(8,128)(2,1)} async-done(((bf16[16,144,2048]{2,1,0:T(8,128)(2,1)}), bf16[16,144,2048]{2,1,0:T(8,128)(2,1)}, u32[]{:S(2)}, u32[]{:S(2)}) %all-to-all-start) | async-done | bytes 9437216 | tf_op jit(solution)/shard_map/all_to_all | solution.py:19
  169.3 5.1 fusion.32
  175.1 9.9 %collective-permute-start = (bf16[128,2048]{1,0:T(8,128)(2,1)S(1)}, bf16[128,2048]{1,0:T(8,128)(2,1)}, u32[]{:S(2)}, u32[]{:S(2)}) collective-permute-start(bf16[128,2048]{1,0:T(8,128)(2,1)S(1)} %pad_maximum_fusion.1), channel_id=1, source_target_pairs={{0,128},{16,144},{32,160},{48,176},{64,192},{80,208},{96,224},{112... | collective-permute-start | bytes 1572872 | tf_op jit(solution)/shard_map/ppermute | solution.py:31
  187.2 4.6 collective-permute-start.2
  196.7 54.4 %collective-permute-start.3 = (bf16[128,2048]{1,0:T(8,128)(2,1)S(1)}, bf16[128,2048]{1,0:T(8,128)(2,1)S(1)}, u32[]{:S(2)}, u32[]{:S(2)}) collective-permute-start(bf16[128,2048]{1,0:T(8,128)(2,1)S(1)} %pad_maximum_fusion.1), channel_id=1, source_target_pairs={{0,80},{16,96},{32,112},{48,128},{64,144},{80,160},{96,176},{112,1... | collective-permute-start | bytes 1572872 | tf_op jit(solution)/shard_map/ppermute | solution.py:31
  253.1 11.7 %collective-permute-start.4 = (bf16[128,2048]{1,0:T(8,128)(2,1)S(1)}, bf16[128,2048]{1,0:T(8,128)(2,1)S(1)}, u32[]{:S(2)}, u32[]{:S(2)}) collective-permute-start(bf16[128,2048]{1,0:T(8,128)(2,1)S(1)} %pad_maximum_fusion.1), channel_id=1, source_target_pairs={{0,64},{16,80},{32,96},{48,112},{64,128},{80,144},{96,160},{112,17... | collective-permute-start | bytes 1572872 | tf_op jit(solution)/shard_map/ppermute | solution.py:31
  270.9 3.3 collective-permute-done.4
  275.0 5.3 collective-permute-done.5
  283.7 6.7 copy.70
  296.2 72.9 %while.20 = (s32[]{:T(128)}, bf16[128,2048]{1,0:T(8,128)(2,1)}, f32[1152,1024]{0,1:T(8,128)}, f32[1152,1024]{0,1:T(8,128)}, bf16[1152,2048]{0,1:T(8,128)(2,1)}, ...) while((s32[]{:T(128)}, bf16[128,2048]{1,0:T(8,128)(2,1)}, ...), condition=%wide.region_6.7_spmd.clone, body=%wide.region_4.6_spmd.clone.sunk | while | flops 766655488 | bytes 39024268 | solution.py:121
  306.5 3.1 fusion.87
  324.8 3.1 fusion.87
  361.2 3.1 fusion.87
  386.8 46.3 %collective-permute-done.9 = bf16[128,2048]{0,1:T(8,128)(2,1)S(1)} collective-permute-done((bf16[128,2048]{0,1:T(8,128)(2,1)S(1)}, bf16[128,2048]{0,1:T(8,128)(2,1)S(1)}, u32[]{:S(2)}, u32[]{:S(2)}) %collective-permute-start.9) | collective-permute-done | bytes 524320 | tf_op jit(solution)/shard_map/ppermute | solution.py:31
  438.6 62.6 %collective-permute-done.11 = bf16[128,2048]{0,1:T(8,128)(2,1)S(1)} collective-permute-done((bf16[128,2048]{0,1:T(8,128)(2,1)S(1)}, bf16[128,2048]{0,1:T(8,128)(2,1)S(1)}, u32[]{:S(2)}, u32[]{:S(2)}) %collective-permute-start.11) | collective-permute-done | bytes 524320 | tf_op jit(solution)/shard_map/ppermute | solution.py:31
  501.2 13.8 %collective-permute-done.12 = bf16[128,2048]{0,1:T(8,128)(2,1)S(1)} collective-permute-done((bf16[128,2048]{0,1:T(8,128)(2,1)S(1)}, bf16[128,2048]{0,1:T(8,128)(2,1)S(1)}, u32[]{:S(2)}, u32[]{:S(2)}) %collective-permute-start.12) | collective-permute-done | bytes 524320 | tf_op jit(solution)/shard_map/ppermute | solution.py:31
  515.0 47.1 %collective-permute-done.13 = bf16[128,2048]{0,1:T(8,128)(2,1)S(1)} collective-permute-done((bf16[128,2048]{0,1:T(8,128)(2,1)S(1)}, bf16[128,2048]{0,1:T(8,128)(2,1)S(1)}, u32[]{:S(2)}, u32[]{:S(2)}) %collective-permute-start.13) | collective-permute-done | bytes 524320 | tf_op jit(solution)/shard_map/ppermute | solution.py:31
  565.2 6.5 fusion.22
  571.8 12.7 %copy.97 = bf16[2304,2048]{1,0:T(8,128)(2,1)} copy(bf16[2304,2048]{0,1:T(8,128)(2,1)} %fusion.22) | data formatting | bytes 18874368
  584.5 171.0 %reduce-scatter.7.cloned.1.call-done = bf16[144,2048]{1,0:T(8,128)(2,1)} async-done(((bf16[2304,2048]{1,0:T(8,128)(2,1)}), bf16[144,2048]{1,0:T(8,128)(2,1)}) %reduce-scatter.7.cloned.1.call-update) | async-done | bytes 589840
  757.8 7.8 fusion.23
  765.6 49.9 %reduce-scatter.5.cloned.1.call-done = bf16[144,128]{0,1:T(8,128)(2,1)} async-done(((bf16[144,2048]{0,1:T(8,128)(2,1)}), bf16[144,128]{0,1:T(8,128)(2,1)}) %reduce-scatter.5.cloned.1.call-update) | async-done | bytes 36880 | tf_op jit(solution)/shard_map/reduce_scatter | solution.py:184
  (179 shorter events, 121.9 us)
Async XLA Ops:
  7.2 162.1 %copy-start = (bf16[1,128,2304]{2,1,0:T(8,128)(2,1)S(1)}, bf16[1,128,2304]{2,1,0:T(8,128)(2,1)}, u32[]{:S(2)}) copy-start(bf16[1,128,2304]{2,1,0:T(8,128)(2,1)} %param.7) | copy-start | bytes 1769476
  13.2 156.2 %all-to-all-start = ((bf16[16,144,2048]{2,1,0:T(8,128)(2,1)}), bf16[16,144,2048]{2,1,0:T(8,128)(2,1)}, u32[]{:S(2)}, u32[]{:S(2)}) async-start(bf16[16,144,2048]{2,1,0:T(8,128)(2,1)} %stack.2), calls=%async_computation | async-start | bytes 18874368 | tf_op jit(solution)/shard_map/all_to_all | solution.py:19
  20.7 734.9 %reduce-scatter.7.cloned.1.call-start = ((), (), s32[]{:S(2)}) async-start(), calls=%async_computation.4 | async-start | bytes 10027008
  23.8 150.8 %copy-start.6 = (f32[128,64]{1,0:T(8,128)}, f32[128,64]{1,0:T(8,128)S(1)}, u32[]{:S(2)}) copy-start(f32[128,64]{1,0:T(8,128)S(1)} %get-tuple-element.364) | copy-start | bytes 98308
  174.4 18.3 %copy-start.9 = (bf16[1,128,2048]{2,1,0:T(8,128)(2,1)S(1)}, bf16[1,128,2048]{2,1,0:T(8,128)(2,1)}, u32[]{:S(2)}) copy-start(bf16[1,128,2048]{2,1,0:T(8,128)(2,1)} %param.11) | copy-start | bytes 1572868
  175.1 21.6 %collective-permute-start = (bf16[128,2048]{1,0:T(8,128)(2,1)S(1)}, bf16[128,2048]{1,0:T(8,128)(2,1)}, u32[]{:S(2)}, u32[]{:S(2)}) collective-permute-start(bf16[128,2048]{1,0:T(8,128)(2,1)S(1)} %pad_maximum_fusion.1), channel_id=1, source_target_pairs={{0,128},{16,144},{32,160},{48,176},{64,192},{80,208},{96,224},{112... | collective-permute-start | bytes 1572872 | tf_op jit(solution)/shard_map/ppermute | solution.py:31
  185.0 68.1 %collective-permute-start.1 = (bf16[128,2048]{1,0:T(8,128)(2,1)S(1)}, bf16[128,2048]{1,0:T(8,128)(2,1)}, u32[]{:S(2)}, u32[]{:S(2)}) collective-permute-start(bf16[128,2048]{1,0:T(8,128)(2,1)S(1)} %pad_maximum_fusion.1), channel_id=1, source_target_pairs={{0,112},{16,128},{32,144},{48,160},{64,176},{80,192},{96,208},{112... | collective-permute-start | bytes 1572872 | tf_op jit(solution)/shard_map/ppermute | solution.py:31
  187.2 79.4 %collective-permute-start.2 = (bf16[128,2048]{1,0:T(8,128)(2,1)S(1)}, bf16[128,2048]{1,0:T(8,128)(2,1)}, u32[]{:S(2)}, u32[]{:S(2)}) collective-permute-start(bf16[128,2048]{1,0:T(8,128)(2,1)S(1)} %pad_maximum_fusion.1), channel_id=1, source_target_pairs={{0,96},{16,112},{32,128},{48,144},{64,160},{80,176},{96,192},{112,... | collective-permute-start | bytes 1572872 | tf_op jit(solution)/shard_map/ppermute | solution.py:31
  193.8 88.3 %collective-permute-start.7 = (bf16[128,2048]{1,0:T(8,128)(2,1)S(1)}, bf16[128,2048]{1,0:T(8,128)(2,1)S(1)}, u32[]{:S(2)}, u32[]{:S(2)}) collective-permute-start(bf16[128,2048]{1,0:T(8,128)(2,1)S(1)} %pad_maximum_fusion.1), channel_id=1, source_target_pairs={{0,16},{16,32},{32,48},{48,64},{64,80},{80,96},{96,112},{112,128},... | collective-permute-start | bytes 1572872 | tf_op jit(solution)/shard_map/ppermute | solution.py:31
  195.1 86.1 %collective-permute-start.6 = (bf16[128,2048]{1,0:T(8,128)(2,1)S(1)}, bf16[128,2048]{1,0:T(8,128)(2,1)S(1)}, u32[]{:S(2)}, u32[]{:S(2)}) collective-permute-start(bf16[128,2048]{1,0:T(8,128)(2,1)S(1)} %pad_maximum_fusion.1), channel_id=1, source_target_pairs={{0,32},{16,48},{32,64},{48,80},{64,96},{80,112},{96,128},{112,144}... | collective-permute-start | bytes 1572872 | tf_op jit(solution)/shard_map/ppermute | solution.py:31
  196.7 73.3 %collective-permute-start.3 = (bf16[128,2048]{1,0:T(8,128)(2,1)S(1)}, bf16[128,2048]{1,0:T(8,128)(2,1)S(1)}, u32[]{:S(2)}, u32[]{:S(2)}) collective-permute-start(bf16[128,2048]{1,0:T(8,128)(2,1)S(1)} %pad_maximum_fusion.1), channel_id=1, source_target_pairs={{0,80},{16,96},{32,112},{48,128},{64,144},{80,160},{96,176},{112,1... | collective-permute-start | bytes 1572872 | tf_op jit(solution)/shard_map/ppermute | solution.py:31
  253.1 21.1 %collective-permute-start.4 = (bf16[128,2048]{1,0:T(8,128)(2,1)S(1)}, bf16[128,2048]{1,0:T(8,128)(2,1)S(1)}, u32[]{:S(2)}, u32[]{:S(2)}) collective-permute-start(bf16[128,2048]{1,0:T(8,128)(2,1)S(1)} %pad_maximum_fusion.1), channel_id=1, source_target_pairs={{0,64},{16,80},{32,96},{48,112},{64,128},{80,144},{96,160},{112,17... | collective-permute-start | bytes 1572872 | tf_op jit(solution)/shard_map/ppermute | solution.py:31
  266.7 13.7 %collective-permute-start.5 = (bf16[128,2048]{1,0:T(8,128)(2,1)S(1)}, bf16[128,2048]{1,0:T(8,128)(2,1)S(1)}, u32[]{:S(2)}, u32[]{:S(2)}) collective-permute-start(bf16[128,2048]{1,0:T(8,128)(2,1)S(1)} %pad_maximum_fusion.1), channel_id=1, source_target_pairs={{0,48},{16,64},{32,80},{48,96},{64,112},{80,128},{96,144},{112,160... | collective-permute-start | bytes 1572872 | tf_op jit(solution)/shard_map/ppermute | solution.py:31
  376.9 8.5 %collective-permute-start.8 = (bf16[128,2048]{0,1:T(8,128)(2,1)S(1)}, bf16[128,2048]{0,1:T(8,128)(2,1)S(1)}, u32[]{:S(2)}, u32[]{:S(2)}) collective-permute-start(bf16[128,2048]{0,1:T(8,128)(2,1)S(1)} %get-tuple-element.348), channel_id=1, source_target_pairs={{16,0},{32,16},{48,32},{64,48},{80,64},{96,80},{112,96},{128,112},... | collective-permute-start | bytes 1572872 | tf_op jit(solution)/shard_map/ppermute | solution.py:31
  378.2 54.9 %collective-permute-start.9 = (bf16[128,2048]{0,1:T(8,128)(2,1)S(1)}, bf16[128,2048]{0,1:T(8,128)(2,1)S(1)}, u32[]{:S(2)}, u32[]{:S(2)}) collective-permute-start(bf16[128,2048]{0,1:T(8,128)(2,1)S(1)} %get-tuple-element.349), channel_id=1, source_target_pairs={{32,0},{48,16},{64,32},{80,48},{96,64},{112,80},{128,96},{144,112}... | collective-permute-start | bytes 1572872 | tf_op jit(solution)/shard_map/ppermute | solution.py:31
  379.5 55.4 %collective-permute-start.10 = (bf16[128,2048]{0,1:T(8,128)(2,1)S(1)}, bf16[128,2048]{0,1:T(8,128)(2,1)S(1)}, u32[]{:S(2)}, u32[]{:S(2)}) collective-permute-start(bf16[128,2048]{0,1:T(8,128)(2,1)S(1)} %get-tuple-element.350), channel_id=1, source_target_pairs={{48,0},{64,16},{80,32},{96,48},{112,64},{128,80},{144,96},{160,112... | collective-permute-start | bytes 1572872 | tf_op jit(solution)/shard_map/ppermute | solution.py:31
  380.8 120.4 %collective-permute-start.11 = (bf16[128,2048]{0,1:T(8,128)(2,1)S(1)}, bf16[128,2048]{0,1:T(8,128)(2,1)S(1)}, u32[]{:S(2)}, u32[]{:S(2)}) collective-permute-start(bf16[128,2048]{0,1:T(8,128)(2,1)S(1)} %get-tuple-element.351), channel_id=1, source_target_pairs={{64,0},{80,16},{96,32},{112,48},{128,64},{144,80},{160,96},{176,11... | collective-permute-start | bytes 1572872 | tf_op jit(solution)/shard_map/ppermute | solution.py:31
  382.1 132.9 %collective-permute-start.12 = (bf16[128,2048]{0,1:T(8,128)(2,1)S(1)}, bf16[128,2048]{0,1:T(8,128)(2,1)S(1)}, u32[]{:S(2)}, u32[]{:S(2)}) collective-permute-start(bf16[128,2048]{0,1:T(8,128)(2,1)S(1)} %get-tuple-element.352), channel_id=1, source_target_pairs={{80,0},{96,16},{112,32},{128,48},{144,64},{160,80},{176,96},{192,1... | collective-permute-start | bytes 1572872 | tf_op jit(solution)/shard_map/ppermute | solution.py:31
  385.5 176.6 %collective-permute-start.13 = (bf16[128,2048]{0,1:T(8,128)(2,1)S(1)}, bf16[128,2048]{0,1:T(8,128)(2,1)S(1)}, u32[]{:S(2)}, u32[]{:S(2)}) collective-permute-start(bf16[128,2048]{0,1:T(8,128)(2,1)S(1)} %get-tuple-element.353), channel_id=1, source_target_pairs={{96,0},{112,16},{128,32},{144,48},{160,64},{176,80},{192,96},{208,... | collective-permute-start | bytes 1572872 | tf_op jit(solution)/shard_map/ppermute | solution.py:31
  433.1 129.0 %collective-permute-start.15 = (bf16[128,2048]{0,1:T(8,128)(2,1)S(1)}, bf16[128,2048]{0,1:T(8,128)(2,1)S(1)}, u32[]{:S(2)}, u32[]{:S(2)}) collective-permute-start(bf16[128,2048]{0,1:T(8,128)(2,1)S(1)} %get-tuple-element.354), channel_id=1, source_target_pairs={{128,0},{144,16},{160,32},{176,48},{192,64},{208,80},{224,96},{240... | collective-permute-start | bytes 1572872 | tf_op jit(solution)/shard_map/ppermute | solution.py:31
  434.9 128.6 %collective-permute-start.14 = (bf16[128,2048]{0,1:T(8,128)(2,1)S(1)}, bf16[128,2048]{0,1:T(8,128)(2,1)S(1)}, u32[]{:S(2)}, u32[]{:S(2)}) collective-permute-start(bf16[128,2048]{0,1:T(8,128)(2,1)S(1)} %get-tuple-element.355), channel_id=1, source_target_pairs={{112,0},{128,16},{144,32},{160,48},{176,64},{192,80},{208,96},{224... | collective-permute-start | bytes 1572872 | tf_op jit(solution)/shard_map/ppermute | solution.py:31
  438.6 126.1 %copy-start.7 = (f32[128,64]{1,0:T(8,128)S(1)}, f32[128,64]{1,0:T(8,128)}, u32[]{:S(2)}) copy-start(f32[128,64]{1,0:T(8,128)} %copy-done.6) | copy-start | bytes 98308
  438.6 126.1 %copy-start.10 = (f32[128,64]{1,0:T(8,128)S(1)}, f32[128,64]{1,0:T(8,128)}, u32[]{:S(2)}) copy-start(f32[128,64]{1,0:T(8,128)} %get-tuple-element.362) | copy-start | bytes 98308
  584.5 231.0 %reduce-scatter.5.cloned.1.call-start = ((), (), s32[]{:S(2)}) async-start(), calls=%async_computation.3 | async-start | bytes 1114112 | tf_op jit(solution)/shard_map/reduce_scatter | solution.py:184
  (26 other events, 97.1 us)
Sparse Core Ops, SparseCore 0:
  584.6 170.9 reduce-scatter.6
  758.3 57.2 reduce-scatter.4
